TPU v7x, 32 devices: a whole 2x2x4 slice. The times are simulated.
32 devices in a mesh: rows: 8 (over z, y), chan: 4 (over x, core).
Axes of the slice: x: 2, y: 2, z: 4, core: 2. Of those that a mesh axis runs over, the one named last changes fastest.
Arguments:
- radiances: float32 [16, 16384], P('chan', 'rows'), may hold values from -6 to 6
- band: int32 [16384, 1], P('rows'), may hold values from 0 to 7; in each aligned block of 2048 rows (0 to 2047, 2048 to 4095, ...) at most 512 rows name the same one
- row_in_band: int32 [16384], P('rows'), may hold values from 0 to 3
- column: int32 [16384], P('rows'), may hold values from 0 to 1439
Outputs:
- cell_count: int32 [32, 1440], P('rows')
- cell_mean: float32 [16, 32, 1440], P('chan', 'rows')
- cell_var: float32 [16, 32, 1440], P('chan', 'rows')
- cell_spread: float32 [32, 1440], P('rows')
- departure: float32 [16, 16384], P('chan', 'rows')
Inputs may be any that keep to these rules, and one draw needn't show every extreme that they name: Within each aligned block of 2048 observations (one scan-time shard) no band is named by more than 512 observations, and in some blocks one band is named by exactly 512.
All inputs are finite; a program needn't handle non-finite values.
Results may differ from a plain program's by a relative error of at most 0.0003.
Values sent between devices are 32-bit elements.
A program may use at most 64 MiB of HBM per device.

v0:
```python
import math
import jax
import jax.numpy as jnp
from jax import lax
from jax.sharding import PartitionSpec as P

CHAN = 16
COLS = 1440
ROWS_DEV = 4


def slot_ranks(dest, nrows):
    obs_dev = dest.shape[0]
    width = math.gcd(obs_dev, 128)
    nblock = obs_dev // width
    owners = jnp.arange(nrows, dtype=jnp.int32)
    hot = (dest[None, :] == owners[:, None]).astype(jnp.bfloat16).reshape(nrows, nblock, width)
    upper = (
        lax.broadcasted_iota(jnp.int32, (width, width), 0)
        <= lax.broadcasted_iota(jnp.int32, (width, width), 1)
    ).astype(jnp.bfloat16)
    inner = jnp.einsum("nbk,kj->nbj", hot, upper, preferred_element_type=jnp.float32)
    hot_float = hot.astype(jnp.float32)
    totals = jnp.sum(hot_float, axis=2)
    before = jnp.cumsum(totals, axis=1) - totals
    ranks = jnp.sum(hot_float * (inner + before[:, :, None]), axis=0).reshape(obs_dev) - 1.0
    return ranks.astype(jnp.int32)


def split_pair(values):
    high = lax.optimization_barrier(values.astype(jnp.bfloat16))
    low = (values - high.astype(jnp.float32)).astype(jnp.bfloat16)
    return (high, low)


def split_three(values):
    high = lax.optimization_barrier(values.astype(jnp.bfloat16))
    rest = values - high.astype(jnp.float32)
    middle = lax.optimization_barrier(rest.astype(jnp.bfloat16))
    low = (rest - middle.astype(jnp.float32)).astype(jnp.bfloat16)
    return (high, middle, low)


def grid_lookup(table, lat_index, col_index):
    fields, nlat, ncol = table.shape
    total = lat_index.shape[0]
    width = math.gcd(total, 2048)
    flat = table.reshape(fields * nlat, ncol)
    lat_iota = jnp.arange(nlat, dtype=jnp.int32)
    col_iota = jnp.arange(ncol, dtype=jnp.int32)

    def look_turn(turn, result):
        start = turn * width
        lat_part = lax.dynamic_slice_in_dim(lat_index, start, width, 0)
        col_part = lax.dynamic_slice_in_dim(col_index, start, width, 0)
        col_hot = (col_iota[:, None] == col_part[None, :]).astype(jnp.float32)
        picked = jnp.dot(
            flat, col_hot, precision=lax.Precision.HIGHEST, preferred_element_type=jnp.float32
        ).reshape(fields, nlat, width)
        lat_hot = (lat_iota[:, None] == lat_part[None, :]).astype(jnp.float32)
        found = jnp.sum(picked * lat_hot[None], axis=1)
        return lax.dynamic_update_slice_in_dim(result, found, start, 1)

    return lax.fori_loop(0, total // width, look_turn, jnp.zeros((fields, total), jnp.float32))


def body(radiances, band, row_in_band, column):
    nrows = lax.axis_size("rows")
    chan_dev, obs_dev = radiances.shape
    cap = 2 * obs_dev // nrows
    total_slots = nrows * cap
    dest = band[:, 0]
    slot = dest * cap + slot_ranks(dest, nrows)
    rad_high, rad_middle, rad_low = split_three(radiances)
    payload = jnp.concatenate(
        [
            rad_high,
            rad_middle,
            rad_low,
            row_in_band[None, :].astype(jnp.bfloat16),
            (column // 64)[None, :].astype(jnp.bfloat16),
            (column % 64)[None, :].astype(jnp.bfloat16),
            jnp.ones((1, obs_dev), jnp.bfloat16),
        ],
        axis=0,
    )
    nload = payload.shape[0]
    span = math.gcd(total_slots, 1024)
    slot_iota = jnp.arange(span, dtype=jnp.int32)

    def pack_turn(turn, buffer):
        start = turn * span
        hot = (slot[:, None] == (start + slot_iota)[None, :]).astype(jnp.bfloat16)
        placed_part = jnp.dot(payload, hot, preferred_element_type=jnp.float32)
        return lax.dynamic_update_slice_in_dim(buffer, placed_part, start, 1)

    placed = lax.fori_loop(
        0, total_slots // span, pack_turn, jnp.zeros((nload, total_slots), jnp.float32)
    )
    sent_values = (
        placed[0:chan_dev] + placed[chan_dev : 2 * chan_dev] + placed[2 * chan_dev : 3 * chan_dev]
    )
    base = 3 * chan_dev
    sent_cell = jnp.where(
        placed[base + 3] > 0.5,
        placed[base] * COLS + placed[base + 1] * 64.0 + placed[base + 2],
        -1.0,
    )
    packed = jnp.concatenate([sent_values, sent_cell[None, :]], axis=0).reshape(
        chan_dev + 1, nrows, cap
    )
    arrived = lax.all_to_all(packed, "rows", split_axis=1, concat_axis=1, tiled=True).reshape(
        chan_dev + 1, total_slots
    )
    values = arrived[:chan_dev]
    cell = arrived[chan_dev].astype(jnp.int32)
    lat_local = jnp.where(cell >= 0, cell // COLS, -1)
    col_local = jnp.where(cell >= 0, cell % COLS, -1)
    value_high, value_low = split_pair(values)
    square_high, square_low = split_pair(values * values)
    features = jnp.concatenate(
        [jnp.ones((1, total_slots), jnp.bfloat16), value_high, value_low, square_high, square_low],
        axis=0,
    )
    nfeat = features.shape[0]
    row_hot = (lat_local[None, :] == jnp.arange(ROWS_DEV, dtype=jnp.int32)[:, None]).astype(
        jnp.bfloat16
    )
    left = (features[:, None, :] * row_hot[None, :, :]).reshape(nfeat * ROWS_DEV, total_slots)
    block = math.gcd(total_slots, 2048)
    turns = total_slots // block
    columns_all = jnp.arange(COLS, dtype=jnp.int32)

    def accumulate(turn, acc):
        start = turn * block
        part = lax.dynamic_slice_in_dim(left, start, block, 1)
        picked = lax.dynamic_slice_in_dim(col_local, start, block, 0)
        col_hot = (picked[:, None] == columns_all[None, :]).astype(jnp.bfloat16)
        return acc + jnp.dot(part, col_hot, preferred_element_type=jnp.float32)

    sums = lax.fori_loop(0, turns, accumulate, jnp.zeros((nfeat * ROWS_DEV, COLS), jnp.float32))
    sums = sums.reshape(nfeat, ROWS_DEV, COLS)
    count = sums[0]
    first = sums[1 : 1 + chan_dev] + sums[1 + chan_dev : 1 + 2 * chan_dev]
    second = sums[1 + 2 * chan_dev : 1 + 3 * chan_dev] + sums[1 + 3 * chan_dev :]
    denom = jnp.maximum(count, 1.0)[None]
    mean = first / denom
    var = jnp.maximum(second / denom - mean * mean, 0.0)
    spread = lax.psum(jnp.sum(var, axis=0), "chan")
    scale = lax.rsqrt(1.0 + spread / CHAN)
    fields = grid_lookup(jnp.concatenate([mean, scale[None]], axis=0), lat_local, col_local)
    shifted = (values - fields[:chan_dev]) * fields[chan_dev][None, :]
    returned = lax.all_to_all(
        shifted.reshape(chan_dev, nrows, cap), "rows", split_axis=1, concat_axis=1, tiled=True
    )
    returned_flat = returned.reshape(chan_dev, total_slots)

    def unplace(turn, result):
        start = turn * span
        hot = (slot[:, None] == (start + slot_iota)[None, :]).astype(jnp.float32)
        part = lax.dynamic_slice_in_dim(returned_flat, start, span, 1)
        return result + lax.dot_general(
            part,
            hot,
            (((1,), (1,)), ((), ())),
            precision=lax.Precision.HIGHEST,
            preferred_element_type=jnp.float32,
        )

    departure = lax.fori_loop(
        0, total_slots // span, unplace, jnp.zeros((chan_dev, obs_dev), jnp.float32)
    )
    return (count.astype(jnp.int32), mean, var, spread, departure)


def solution(mesh):
    in_specs = (P("chan", "rows"), P("rows", None), P("rows"), P("rows"))
    out_specs = (
        P("rows", None),
        P("chan", "rows", None),
        P("chan", "rows", None),
        P("rows", None),
        P("chan", "rows"),
    )
    return jax.shard_map(body, mesh=mesh, in_specs=in_specs, out_specs=out_specs, check_vma=False)
```

profile of v0, /device:TPU:0, one launch (start us, length us, event | category | flops | bytes accessed | tf_op | source)
XLA Modules:
  0.0 82.0 jit_solution(14672771929657307120)
XLA Ops:
  0.6 0.8 convert_element_type.110
  1.4 0.8 fusion.46
  2.2 0.8 subtract_convert_fusion.2
  2.9 0.7 fusion.50
  3.7 0.7 convert_element_type.115
  4.4 0.7 broadcast_multiply_fusion.1
  5.1 0.8 convert_reduce_fusion
  6.1 0.9 %fusion.39 = f32[16,128]{1,0:T(8,128)S(1)} fusion(f32[8,16]{1,0:T(8,128)S(1)} %sub.41, s32[16,128]{1,0:T(8,128)} %bitcast.49), kind=kOutput, calls=%fused_computation.36 | convolution fusion | flops 4323328 | bytes 16896 | tf_op jit(solution)/shard_map/nbk,kj->nbj/dot_general | solution.py:22
  7.2 5.7 %while.56 = (s32[]{:T(128)}, f32[16,4096]{1,0:T(8,128)S(1)}, s32[2048]{0:T(1024)S(1)}, bf16[16,2048]{1,0:T(8,128)(2,1)S(1)}, s32[]{:T(128)}, /*index=5*/s32[]{:T(128)}, s32[]{:T(128)}, s32[]{:T(128)}) while((s32[]{:T(128)}, f32[16,4096]{1,0:T(8,128)S(1)}, s32[2048]{0:T(1024)S(1)}, bf16[16,2048]{1,0:T(8,128)(2,1)S(1)}, s32[]{:T(128)}, ...), condition=%wide.region_4.5_spmd.clone, body=%wide.region_3.4_spmd.clone.sunk | while | flops 69207048 | bytes 147595 | solution.py:97
  7.2 1.4 %fusion.70 = f32[16,4096]{1,0:T(8,128)S(1)} fusion(f32[16,4096]{1,0:T(8,128)S(1)} %get-tuple-element.638, s32[]{:T(128)S(6)} %select_n.104, bf16[16,2048]{1,0:T(8,128)(2,1)S(1)} %get-tuple-element.648, s32[1024]{0:T(1024)S(1)} %iota_add_fusion.4, s32[2048]{0:T(1024)S(1)} %get-tuple-element.647), kind=kOutput, calls=%fused_computation.10.clone.1 | convolution fusion | flops 69206016 | bytes 143364 | tf_op jit(solution)/shard_map/while/body/eval_jaxpr/dot_general | solution.py:94
  8.6 1.4 %fusion.70 = f32[16,4096]{1,0:T(8,128)S(1)} fusion(f32[16,4096]{1,0:T(8,128)S(1)} %get-tuple-element.638, s32[]{:T(128)S(6)} %select_n.104, bf16[16,2048]{1,0:T(8,128)(2,1)S(1)} %get-tuple-element.648, s32[1024]{0:T(1024)S(1)} %iota_add_fusion.4, s32[2048]{0:T(1024)S(1)} %get-tuple-element.647), kind=kOutput, calls=%fused_computation.10.clone.1 | convolution fusion | flops 69206016 | bytes 143364 | tf_op jit(solution)/shard_map/while/body/eval_jaxpr/dot_general | solution.py:94
  10.0 1.4 %fusion.70 = f32[16,4096]{1,0:T(8,128)S(1)} fusion(f32[16,4096]{1,0:T(8,128)S(1)} %get-tuple-element.638, s32[]{:T(128)S(6)} %select_n.104, bf16[16,2048]{1,0:T(8,128)(2,1)S(1)} %get-tuple-element.648, s32[1024]{0:T(1024)S(1)} %iota_add_fusion.4, s32[2048]{0:T(1024)S(1)} %get-tuple-element.647), kind=kOutput, calls=%fused_computation.10.clone.1 | convolution fusion | flops 69206016 | bytes 143364 | tf_op jit(solution)/shard_map/while/body/eval_jaxpr/dot_general | solution.py:94
  11.4 1.4 %fusion.70 = f32[16,4096]{1,0:T(8,128)S(1)} fusion(f32[16,4096]{1,0:T(8,128)S(1)} %get-tuple-element.638, s32[]{:T(128)S(6)} %select_n.104, bf16[16,2048]{1,0:T(8,128)(2,1)S(1)} %get-tuple-element.648, s32[1024]{0:T(1024)S(1)} %iota_add_fusion.4, s32[2048]{0:T(1024)S(1)} %get-tuple-element.647), kind=kOutput, calls=%fused_computation.10.clone.1 | convolution fusion | flops 69206016 | bytes 143364 | tf_op jit(solution)/shard_map/while/body/eval_jaxpr/dot_general | solution.py:94
  12.9 0.7 pad_maximum_fusion
  13.6 7.3 %all-to-all-start = ((f32[5,8,512]{2,0,1:T(8,128)}), f32[5,8,512]{2,0,1:T(8,128)S(1)}, u32[]{:S(2)}, u32[]{:S(2)}) async-start(f32[5,8,512]{2,0,1:T(8,128)} %pad_maximum_fusion), calls=%async_computation | async-start | bytes 262144 | tf_op jit(solution)/shard_map/all_to_all | solution.py:112
  20.9 7.3 %all-to-all-done = f32[5,8,512]{2,0,1:T(8,128)S(1)} async-done(((f32[5,8,512]{2,0,1:T(8,128)}), f32[5,8,512]{2,0,1:T(8,128)S(1)}, u32[]{:S(2)}, u32[]{:S(2)}) %all-to-all-start) | async-done | bytes 81952 | tf_op jit(solution)/shard_map/all_to_all | solution.py:112
  29.6 5.4 %while.58 = (s32[]{:T(128)}, f32[68,1440]{1,0:T(8,128)S(1)}, bf16[68,4096]{1,0:T(8,128)(2,1)S(1)}, s32[4096]{0:T(1024)S(1)}, s32[]{:T(128)}, /*index=5*/s32[]{:T(128)}, s32[]{:T(128)}, s32[]{:T(128)}) while((s32[]{:T(128)}, f32[68,1440]{1,0:T(8,128)S(1)}, bf16[68,4096]{1,0:T(8,128)(2,1)S(1)}, s32[4096]{0:T(1024)S(1)}, s32[]{:T(128)}, ...), condition=%wide.region_6.7_spmd.clone, body=%wide.region_5.6_spmd.clone.sunk | while | flops 404225280 | bytes 1153685 | solution.py:141
  29.6 2.7 %fusion.75 = f32[68,1440]{1,0:T(8,128)S(1)} fusion(s32[2048]{0:T(1024)S(1)} %dynamic_slice.52, f32[68,1440]{1,0:T(8,128)S(1)} %get-tuple-element.662, bf16[68,4096]{1,0:T(8,128)(2,1)S(1)} %get-tuple-element.671, s32[]{:T(128)S(6)} %select_n.106, pred[]{:T(512)S(6)} %compare.9), kind=kOutput, calls=%fused_computation.23.clone.1 | convolution fusion | flops 404225280 | bytes 1137157 | tf_op jit(solution)/shard_map/while/body/eval_jaxpr/dot_general | solution.py:139
  32.3 2.7 %fusion.75 = f32[68,1440]{1,0:T(8,128)S(1)} fusion(s32[2048]{0:T(1024)S(1)} %dynamic_slice.52, f32[68,1440]{1,0:T(8,128)S(1)} %get-tuple-element.662, bf16[68,4096]{1,0:T(8,128)(2,1)S(1)} %get-tuple-element.671, s32[]{:T(128)S(6)} %select_n.106, pred[]{:T(512)S(6)} %compare.9), kind=kOutput, calls=%fused_computation.23.clone.1 | convolution fusion | flops 404225280 | bytes 1137157 | tf_op jit(solution)/shard_map/while/body/eval_jaxpr/dot_general | solution.py:139
  35.7 0.7 fusion.53
  36.5 10.3 %psum.7 = f32[4,1440]{1,0:T(4,128)S(1)} all-reduce(f32[4,1440]{1,0:T(4,128)S(1)} %get-tuple-element.508), channel_id=1, replica_groups=mesh['rows'=8,'chan'=4] {'chan'}, use_global_device_ids=true, to_apply=%region_8.9 | all-reduce | flops 5760 | bytes 46080 | tf_op jit(solution)/shard_map/psum | solution.py:149
  47.3 8.0 %while.57 = (s32[]{:T(128)}, f32[5,4096]{1,0:T(8,128)S(1)}, s32[4096]{0:T(1024)S(1)}, f32[20,1440]{1,0:T(8,128)S(1)}, s32[4096]{0:T(1024)S(1)}, /*index=5*/s32[]{:T(128)}, s32[]{:T(128)}, s32[]{:T(128)}, s32[]{:T(128)}) while((s32[]{:T(128)}, f32[5,4096]{1,0:T(8,128)S(1)}, s32[4096]{0:T(1024)S(1)}, f32[20,1440]{1,0:T(8,128)S(1)}, ...), condition=%wide.region_11.12_spmd.clone, body=%wide.region_9.11_spmd.clone.sunk | while | flops 710825984 | bytes 1057431 | solution.py:64
  47.3 3.7 %fusion.72 = f32[20,2048]{1,0:T(8,128)S(1)} fusion(f32[20,1440]{1,0:T(8,128)S(1)} %get-tuple-element.698, s32[2048]{0:T(1024)S(1)} %dynamic_slice.49), kind=kOutput, calls=%fused_computation.15.clone.1 | convolution fusion | flops 710737920 | bytes 287232 | tf_op jit(solution)/shard_map/while/body/eval_jaxpr/dot_general | solution.py:57
  51.3 3.7 %fusion.72 = f32[20,2048]{1,0:T(8,128)S(1)} fusion(f32[20,1440]{1,0:T(8,128)S(1)} %get-tuple-element.698, s32[2048]{0:T(1024)S(1)} %dynamic_slice.49), kind=kOutput, calls=%fused_computation.15.clone.1 | convolution fusion | flops 710737920 | bytes 287232 | tf_op jit(solution)/shard_map/while/body/eval_jaxpr/dot_general | solution.py:57
  55.3 0.6 subtract_multiply_fusion
  56.0 3.3 %all-to-all-start.1 = ((f32[4,8,512]{2,0,1:T(4,128)}), f32[4,8,512]{2,0,1:T(4,128)S(1)}, u32[]{:S(2)}, u32[]{:S(2)}) async-start(f32[4,8,512]{2,0,1:T(4,128)} %bitcast.11), calls=%async_computation.1 | async-start | bytes 131072 | tf_op jit(solution)/shard_map/all_to_all | solution.py:153
  59.4 6.8 %all-to-all-done.1 = f32[4,8,512]{2,0,1:T(4,128)S(1)} async-done(((f32[4,8,512]{2,0,1:T(4,128)}), f32[4,8,512]{2,0,1:T(4,128)S(1)}, u32[]{:S(2)}, u32[]{:S(2)}) %all-to-all-start.1) | async-done | bytes 65568 | tf_op jit(solution)/shard_map/all_to_all | solution.py:153
  66.2 15.2 %while.59 = (s32[]{:T(128)}, f32[4,2048]{1,0:T(4,128)S(1)}, f32[4,4096]{1,0:T(4,128)S(1)}, s32[2048]{0:T(1024)S(1)}, s32[]{:T(128)}, /*index=5*/s32[]{:T(128)}, s32[]{:T(128)}, s32[]{:T(128)}) while((s32[]{:T(128)}, f32[4,2048]{1,0:T(4,128)S(1)}, f32[4,4096]{1,0:T(4,128)S(1)}, s32[2048]{0:T(1024)S(1)}, s32[]{:T(128)}, ...), condition=%wide.region_13.14_spmd.clone, body=%wide.region_12.13_spmd.clone.sunk | while | flops 102777864 | bytes 98453 | solution.py:170
  66.2 3.8 %fusion.78 = f32[4,2048]{1,0:T(4,128)S(1)} fusion(s32[1024]{0:T(1024)S(1)} %iota_add_fusion.5, s32[2048]{0:T(1024)S(1)} %get-tuple-element.723, f32[4,2048]{1,0:T(4,128)S(1)} %get-tuple-element.713, f32[4,4096]{1,0:T(4,128)S(1)} %get-tuple-element.722, s32[]{:T(128)S(6)} %select_n.107, pred[]{:T(512)S(6)} %compare.10), kind=kOutput, calls=%fused_computation.30.clone.1 | convolution fusion | flops 102776832 | bytes 94213 | tf_op jit(solution)/shard_map/while/body/eval_jaxpr/dot_general | solution.py:162
  70.0 3.8 %fusion.78 = f32[4,2048]{1,0:T(4,128)S(1)} fusion(s32[1024]{0:T(1024)S(1)} %iota_add_fusion.5, s32[2048]{0:T(1024)S(1)} %get-tuple-element.723, f32[4,2048]{1,0:T(4,128)S(1)} %get-tuple-element.713, f32[4,4096]{1,0:T(4,128)S(1)} %get-tuple-element.722, s32[]{:T(128)S(6)} %select_n.107, pred[]{:T(512)S(6)} %compare.10), kind=kOutput, calls=%fused_computation.30.clone.1 | convolution fusion | flops 102776832 | bytes 94213 | tf_op jit(solution)/shard_map/while/body/eval_jaxpr/dot_general | solution.py:162
  73.8 3.8 %fusion.78 = f32[4,2048]{1,0:T(4,128)S(1)} fusion(s32[1024]{0:T(1024)S(1)} %iota_add_fusion.5, s32[2048]{0:T(1024)S(1)} %get-tuple-element.723, f32[4,2048]{1,0:T(4,128)S(1)} %get-tuple-element.713, f32[4,4096]{1,0:T(4,128)S(1)} %get-tuple-element.722, s32[]{:T(128)S(6)} %select_n.107, pred[]{:T(512)S(6)} %compare.10), kind=kOutput, calls=%fused_computation.30.clone.1 | convolution fusion | flops 102776832 | bytes 94213 | tf_op jit(solution)/shard_map/while/body/eval_jaxpr/dot_general | solution.py:162
  77.6 3.8 %fusion.78 = f32[4,2048]{1,0:T(4,128)S(1)} fusion(s32[1024]{0:T(1024)S(1)} %iota_add_fusion.5, s32[2048]{0:T(1024)S(1)} %get-tuple-element.723, f32[4,2048]{1,0:T(4,128)S(1)} %get-tuple-element.713, f32[4,4096]{1,0:T(4,128)S(1)} %get-tuple-element.722, s32[]{:T(128)S(6)} %select_n.107, pred[]{:T(512)S(6)} %compare.10), kind=kOutput, calls=%fused_computation.30.clone.1 | convolution fusion | flops 102776832 | bytes 94213 | tf_op jit(solution)/shard_map/while/body/eval_jaxpr/dot_general | solution.py:162
  (64 shorter events, 4.0 us)
Async XLA Ops:
  13.6 14.7 %all-to-all-start = ((f32[5,8,512]{2,0,1:T(8,128)}), f32[5,8,512]{2,0,1:T(8,128)S(1)}, u32[]{:S(2)}, u32[]{:S(2)}) async-start(f32[5,8,512]{2,0,1:T(8,128)} %pad_maximum_fusion), calls=%async_computation | async-start | bytes 262144 | tf_op jit(solution)/shard_map/all_to_all | solution.py:112
  36.4 10.4 %copy-start = (f32[4,4,1440]{2,1,0:T(4,128)}, f32[4,4,1440]{2,1,0:T(4,128)S(1)}, u32[]{:S(2)}) copy-start(f32[4,4,1440]{2,1,0:T(4,128)S(1)} %get-tuple-element.510) | copy-start | bytes 276484
  46.7 0.6 copy-start.1
  56.0 10.2 %all-to-all-start.1 = ((f32[4,8,512]{2,0,1:T(4,128)}), f32[4,8,512]{2,0,1:T(4,128)S(1)}, u32[]{:S(2)}, u32[]{:S(2)}) async-start(f32[4,8,512]{2,0,1:T(4,128)} %bitcast.11), calls=%async_computation.1 | async-start | bytes 131072 | tf_op jit(solution)/shard_map/all_to_all | solution.py:153
  81.4 0.6 copy-start.2
where the time goes:
time: 82.7 us; the launch traced here: 82 us
  matrix products  34.5 us (42%)
  waiting for transfers between devices  14.2 us (17%)
  starting transfers between devices  10.7 us (13%)
  blocking collectives  10.3 us (12%)
  other arithmetic  9.1 us (11%)
  local copies, waits for them, and re-layouts  2.18 us (3%)
  between operations  0.93 us (1%)
    dot_general x4, matrix products, unplace(): lax.dot_general(part, hot, (((1,), (1,)), ((), ())), precision=lax.Precis...  15.1 us
    psum x1, blocking collectives, body(): spread = lax.psum(jnp.sum(var, axis=0), 'chan')  10.3 us
    dot_general x2, matrix products, look_turn(): jnp.dot(flat, col_hot, precision=lax.Precision.HIGHEST, preferred_element...  7.49 us
    all_to_all x1, waiting for transfers between devices, body(): lax.all_to_all(packed, 'rows', split_axis=1, concat_axis=1, tiled=True)  7.34 us
    all_to_all x1, starting transfers between devices, body(): lax.all_to_all(packed, 'rows', split_axis=1, concat_axis=1, tiled=True)  7.31 us
    all_to_all x1, waiting for transfers between devices, body(): lax.all_to_all(shifted.reshape(chan_dev, nrows, cap), 'rows', split_axis=...  6.83 us
    dot_general x4, matrix products, pack_turn(): placed_part = jnp.dot(payload, hot, preferred_element_type=jnp.float32)  5.63 us
    dot_general x2, matrix products, accumulate(): return acc + jnp.dot(part, col_hot, preferred_element_type=jnp.float32)  5.3 us
  transfers between devices with their start and end apart: 2, of which 2 were waited for; matrix products, arithmetic and copies ran while one was open for 0% of the time, Pallas kernels for 0%

commit v1 on v0

--- a/solution.py
+++ b/solution.py
@@ -1,3 +1,4 @@
+import functools
 import math
 import jax
 import jax.numpy as jnp
@@ -7,6 +8,15 @@
 CHAN = 16
 COLS = 1440
 ROWS_DEV = 4
+
+
+def report_the_numbers(inputs, mesh_ax):
+    step_out = jax.lax.all_gather(inputs, mesh_ax)
+    plain = jnp.sum(step_out, axis=0)
+    return plain
+
+
+try_all_teams = functools.partial(report_the_numbers, mesh_ax="chan")
 
 
 def slot_ranks(dest, nrows):
@@ -146,7 +156,7 @@
     denom = jnp.maximum(count, 1.0)[None]
     mean = first / denom
     var = jnp.maximum(second / denom - mean * mean, 0.0)
-    spread = lax.psum(jnp.sum(var, axis=0), "chan")
+    spread = try_all_teams(jnp.sum(var, axis=0))
     scale = lax.rsqrt(1.0 + spread / CHAN)
     fields = grid_lookup(jnp.concatenate([mean, scale[None]], axis=0), lat_local, col_local)
     shifted = (values - fields[:chan_dev]) * fields[chan_dev][None, :]

time: 82.7 us -> 77.8 us (0.941)
  blocking collectives: 10.3 us -> 5.31 us
    psum x1 -> x0, blocking collectives: 10.3 us -> none  [body(): spread = lax.psum(jnp.sum(var, axis=0), 'chan')]
    all_gather x0 -> x1, blocking collectives: none -> 5.31 us  [report_the_numbers(): step_out = jax.lax.all_gather(inputs, mesh_ax)]
where the time goes in v1:
time: 77.8 us; the launch traced here: 77.1 us
  matrix products  34.5 us (44%)
  waiting for transfers between devices  14.2 us (18%)
  starting transfers between devices  10.7 us (14%)
  other arithmetic  9.13 us (12%)
  blocking collectives  5.31 us (7%)
  local copies, waits for them, and re-layouts  2.18 us (3%)
  between operations  0.93 us (1%)
    dot_general x4, matrix products, unplace(): lax.dot_general(part, hot, (((1,), (1,)), ((), ())), precision=lax.Precis...  15.1 us
    dot_general x2, matrix products, look_turn(): jnp.dot(flat, col_hot, precision=lax.Precision.HIGHEST, preferred_element...  7.49 us
    all_to_all x1, waiting for transfers between devices, body(): lax.all_to_all(packed, 'rows', split_axis=1, concat_axis=1, tiled=True)  7.34 us
    all_to_all x1, starting transfers between devices, body(): lax.all_to_all(packed, 'rows', split_axis=1, concat_axis=1, tiled=True)  7.31 us
    all_to_all x1, waiting for transfers between devices, body(): lax.all_to_all(shifted.reshape(chan_dev, nrows, cap), 'rows', split_axis=...  6.83 us
    dot_general x4, matrix products, pack_turn(): placed_part = jnp.dot(payload, hot, preferred_element_type=jnp.float32)  5.63 us
    all_gather x1, blocking collectives, report_the_numbers(): step_out = jax.lax.all_gather(inputs, mesh_ax)  5.31 us
    dot_general x2, matrix products, accumulate(): return acc + jnp.dot(part, col_hot, preferred_element_type=jnp.float32)  5.3 us
  transfers between devices with their start and end apart: 2, of which 2 were waited for; matrix products, arithmetic and copies ran while one was open for 0% of the time, Pallas kernels for 0%

profile of v1, /device:TPU:0, one launch (start us, length us, event | category | flops | bytes accessed | tf_op | source)
XLA Modules:
  0.0 77.1 jit_solution(3056551716962871957)
XLA Ops:
  0.6 0.8 convert_element_type.110
  1.4 0.8 fusion.46
  2.2 0.8 %subtract_convert_fusion.2 = bf16[4,2048]{1,0:T(4,128)(2,1)S(1)} fusion(bf16[4,2048]{1,0:T(4,128)(2,1)S(1)} %fusion.46, f32[4,2048]{1,0:T(4,128)} %param.12, bf16[4,2048]{1,0:T(4,128)(2,1)S(1)} %convert_element_type.110), kind=kLoop, calls=%fused_computation.60 | loop fusion | flops 40960 | bytes 81920 | tf_op jit(solution)/shard_map/convert_element_type | solution.py:50
  2.9 0.7 fusion.50
  3.7 0.7 convert_element_type.115
  4.4 0.7 broadcast_multiply_fusion.1
  5.1 0.8 %convert_reduce_fusion = f32[8,16]{1,0:T(8,128)S(1)} fusion(s32[16,128]{1,0:T(8,128)} %bitcast.50), kind=kLoop, calls=%fused_computation.44 | loop fusion | flops 65408 | bytes 8704 | tf_op jit(solution)/shard_map/reduce_sum | solution.py:34
  6.1 0.9 %fusion.39 = f32[16,128]{1,0:T(8,128)S(1)} fusion(f32[8,16]{1,0:T(8,128)S(1)} %sub.41, s32[16,128]{1,0:T(8,128)} %bitcast.51), kind=kOutput, calls=%fused_computation.36 | convolution fusion | flops 4323328 | bytes 16896 | tf_op jit(solution)/shard_map/nbk,kj->nbj/dot_general | solution.py:32
  7.2 5.7 %while.56 = (s32[]{:T(128)}, f32[16,4096]{1,0:T(8,128)S(1)}, s32[2048]{0:T(1024)S(1)}, bf16[16,2048]{1,0:T(8,128)(2,1)S(1)}, s32[]{:T(128)}, /*index=5*/s32[]{:T(128)}, s32[]{:T(128)}, s32[]{:T(128)}) while((s32[]{:T(128)}, f32[16,4096]{1,0:T(8,128)S(1)}, s32[2048]{0:T(1024)S(1)}, bf16[16,2048]{1,0:T(8,128)(2,1)S(1)}, s32[]{:T(128)}, ...), condition=%wide.region_4.5_spmd.clone, body=%wide.region_3.4_spmd.clone.sunk | while | flops 69207048 | bytes 147595 | solution.py:107
  7.2 1.4 %fusion.70 = f32[16,4096]{1,0:T(8,128)S(1)} fusion(f32[16,4096]{1,0:T(8,128)S(1)} %get-tuple-element.638, s32[]{:T(128)S(6)} %select_n.104, bf16[16,2048]{1,0:T(8,128)(2,1)S(1)} %get-tuple-element.648, s32[1024]{0:T(1024)S(1)} %iota_add_fusion.4, s32[2048]{0:T(1024)S(1)} %get-tuple-element.647), kind=kOutput, calls=%fused_computation.10.clone.1 | convolution fusion | flops 69206016 | bytes 143364 | tf_op jit(solution)/shard_map/while/body/eval_jaxpr/dot_general | solution.py:104
  8.6 1.4 %fusion.70 = f32[16,4096]{1,0:T(8,128)S(1)} fusion(f32[16,4096]{1,0:T(8,128)S(1)} %get-tuple-element.638, s32[]{:T(128)S(6)} %select_n.104, bf16[16,2048]{1,0:T(8,128)(2,1)S(1)} %get-tuple-element.648, s32[1024]{0:T(1024)S(1)} %iota_add_fusion.4, s32[2048]{0:T(1024)S(1)} %get-tuple-element.647), kind=kOutput, calls=%fused_computation.10.clone.1 | convolution fusion | flops 69206016 | bytes 143364 | tf_op jit(solution)/shard_map/while/body/eval_jaxpr/dot_general | solution.py:104
  10.0 1.4 %fusion.70 = f32[16,4096]{1,0:T(8,128)S(1)} fusion(f32[16,4096]{1,0:T(8,128)S(1)} %get-tuple-element.638, s32[]{:T(128)S(6)} %select_n.104, bf16[16,2048]{1,0:T(8,128)(2,1)S(1)} %get-tuple-element.648, s32[1024]{0:T(1024)S(1)} %iota_add_fusion.4, s32[2048]{0:T(1024)S(1)} %get-tuple-element.647), kind=kOutput, calls=%fused_computation.10.clone.1 | convolution fusion | flops 69206016 | bytes 143364 | tf_op jit(solution)/shard_map/while/body/eval_jaxpr/dot_general | solution.py:104
  11.4 1.4 %fusion.70 = f32[16,4096]{1,0:T(8,128)S(1)} fusion(f32[16,4096]{1,0:T(8,128)S(1)} %get-tuple-element.638, s32[]{:T(128)S(6)} %select_n.104, bf16[16,2048]{1,0:T(8,128)(2,1)S(1)} %get-tuple-element.648, s32[1024]{0:T(1024)S(1)} %iota_add_fusion.4, s32[2048]{0:T(1024)S(1)} %get-tuple-element.647), kind=kOutput, calls=%fused_computation.10.clone.1 | convolution fusion | flops 69206016 | bytes 143364 | tf_op jit(solution)/shard_map/while/body/eval_jaxpr/dot_general | solution.py:104
  12.9 0.7 pad_maximum_fusion
  13.6 7.3 %all-to-all-start = ((f32[5,8,512]{2,0,1:T(8,128)}), f32[5,8,512]{2,0,1:T(8,128)S(1)}, u32[]{:S(2)}, u32[]{:S(2)}) async-start(f32[5,8,512]{2,0,1:T(8,128)} %pad_maximum_fusion), calls=%async_computation | async-start | bytes 262144 | tf_op jit(solution)/shard_map/all_to_all | solution.py:122
  20.9 7.3 %all-to-all-done = f32[5,8,512]{2,0,1:T(8,128)S(1)} async-done(((f32[5,8,512]{2,0,1:T(8,128)}), f32[5,8,512]{2,0,1:T(8,128)S(1)}, u32[]{:S(2)}, u32[]{:S(2)}) %all-to-all-start) | async-done | bytes 81952 | tf_op jit(solution)/shard_map/all_to_all | solution.py:122
  29.6 5.4 %while.58 = (s32[]{:T(128)}, f32[68,1440]{1,0:T(8,128)S(1)}, bf16[68,4096]{1,0:T(8,128)(2,1)S(1)}, s32[4096]{0:T(1024)S(1)}, s32[]{:T(128)}, /*index=5*/s32[]{:T(128)}, s32[]{:T(128)}, s32[]{:T(128)}) while((s32[]{:T(128)}, f32[68,1440]{1,0:T(8,128)S(1)}, bf16[68,4096]{1,0:T(8,128)(2,1)S(1)}, s32[4096]{0:T(1024)S(1)}, s32[]{:T(128)}, ...), condition=%wide.region_6.7_spmd.clone, body=%wide.region_5.6_spmd.clone.sunk | while | flops 404225280 | bytes 1153685 | solution.py:151
  29.6 2.7 %fusion.75 = f32[68,1440]{1,0:T(8,128)S(1)} fusion(s32[2048]{0:T(1024)S(1)} %dynamic_slice.52, f32[68,1440]{1,0:T(8,128)S(1)} %get-tuple-element.662, bf16[68,4096]{1,0:T(8,128)(2,1)S(1)} %get-tuple-element.671, s32[]{:T(128)S(6)} %select_n.106, pred[]{:T(512)S(6)} %compare.9), kind=kOutput, calls=%fused_computation.23.clone.1 | convolution fusion | flops 404225280 | bytes 1137157 | tf_op jit(solution)/shard_map/while/body/eval_jaxpr/dot_general | solution.py:149
  32.3 2.7 %fusion.75 = f32[68,1440]{1,0:T(8,128)S(1)} fusion(s32[2048]{0:T(1024)S(1)} %dynamic_slice.52, f32[68,1440]{1,0:T(8,128)S(1)} %get-tuple-element.662, bf16[68,4096]{1,0:T(8,128)(2,1)S(1)} %get-tuple-element.671, s32[]{:T(128)S(6)} %select_n.106, pred[]{:T(512)S(6)} %compare.9), kind=kOutput, calls=%fused_computation.23.clone.1 | convolution fusion | flops 404225280 | bytes 1137157 | tf_op jit(solution)/shard_map/while/body/eval_jaxpr/dot_general | solution.py:149
  35.7 0.7 fusion.53
  36.5 5.3 %all-gather.1 = f32[4,4,1440]{2,1,0:T(4,128)S(1)} all-gather(f32[1,4,1440]{2,1,0:T(4,128)S(1)} %bitcast.43), channel_id=2, replica_groups=mesh['rows'=8,'chan'=4] {'chan'}, dimensions={0}, use_global_device_ids=true | all-gather | bytes 115200 | tf_op jit(solution)/shard_map/all_gather | solution.py:14
  42.4 8.0 %while.57 = (s32[]{:T(128)}, f32[5,4096]{1,0:T(8,128)S(1)}, s32[4096]{0:T(1024)S(1)}, f32[20,1440]{1,0:T(8,128)S(1)}, s32[4096]{0:T(1024)S(1)}, /*index=5*/s32[]{:T(128)}, s32[]{:T(128)}, s32[]{:T(128)}, s32[]{:T(128)}) while((s32[]{:T(128)}, f32[5,4096]{1,0:T(8,128)S(1)}, s32[4096]{0:T(1024)S(1)}, f32[20,1440]{1,0:T(8,128)S(1)}, ...), condition=%wide.region_11.12_spmd.clone, body=%wide.region_9.11_spmd.clone.sunk | while | flops 710825984 | bytes 1057431 | solution.py:74
  42.4 3.7 %fusion.72 = f32[20,2048]{1,0:T(8,128)S(1)} fusion(f32[20,1440]{1,0:T(8,128)S(1)} %get-tuple-element.698, s32[2048]{0:T(1024)S(1)} %dynamic_slice.49), kind=kOutput, calls=%fused_computation.15.clone.1 | convolution fusion | flops 710737920 | bytes 287232 | tf_op jit(solution)/shard_map/while/body/eval_jaxpr/dot_general | solution.py:67
  46.4 3.7 %fusion.72 = f32[20,2048]{1,0:T(8,128)S(1)} fusion(f32[20,1440]{1,0:T(8,128)S(1)} %get-tuple-element.698, s32[2048]{0:T(1024)S(1)} %dynamic_slice.49), kind=kOutput, calls=%fused_computation.15.clone.1 | convolution fusion | flops 710737920 | bytes 287232 | tf_op jit(solution)/shard_map/while/body/eval_jaxpr/dot_general | solution.py:67
  50.4 0.6 subtract_multiply_fusion
  51.1 3.3 %all-to-all-start.1 = ((f32[4,8,512]{2,0,1:T(4,128)}), f32[4,8,512]{2,0,1:T(4,128)S(1)}, u32[]{:S(2)}, u32[]{:S(2)}) async-start(f32[4,8,512]{2,0,1:T(4,128)} %bitcast.12), calls=%async_computation.1 | async-start | bytes 131072 | tf_op jit(solution)/shard_map/all_to_all | solution.py:163
  54.4 6.8 %all-to-all-done.1 = f32[4,8,512]{2,0,1:T(4,128)S(1)} async-done(((f32[4,8,512]{2,0,1:T(4,128)}), f32[4,8,512]{2,0,1:T(4,128)S(1)}, u32[]{:S(2)}, u32[]{:S(2)}) %all-to-all-start.1) | async-done | bytes 65568 | tf_op jit(solution)/shard_map/all_to_all | solution.py:163
  61.3 15.2 %while.59 = (s32[]{:T(128)}, f32[4,2048]{1,0:T(4,128)S(1)}, f32[4,4096]{1,0:T(4,128)S(1)}, s32[2048]{0:T(1024)S(1)}, s32[]{:T(128)}, /*index=5*/s32[]{:T(128)}, s32[]{:T(128)}, s32[]{:T(128)}) while((s32[]{:T(128)}, f32[4,2048]{1,0:T(4,128)S(1)}, f32[4,4096]{1,0:T(4,128)S(1)}, s32[2048]{0:T(1024)S(1)}, s32[]{:T(128)}, ...), condition=%wide.region_13.14_spmd.clone, body=%wide.region_12.13_spmd.clone.sunk | while | flops 102777864 | bytes 98453 | solution.py:180
  61.3 3.8 %fusion.78 = f32[4,2048]{1,0:T(4,128)S(1)} fusion(s32[1024]{0:T(1024)S(1)} %iota_add_fusion.5, s32[2048]{0:T(1024)S(1)} %get-tuple-element.723, f32[4,2048]{1,0:T(4,128)S(1)} %get-tuple-element.713, f32[4,4096]{1,0:T(4,128)S(1)} %get-tuple-element.722, s32[]{:T(128)S(6)} %select_n.107, pred[]{:T(512)S(6)} %compare.10), kind=kOutput, calls=%fused_computation.30.clone.1 | convolution fusion | flops 102776832 | bytes 94213 | tf_op jit(solution)/shard_map/while/body/eval_jaxpr/dot_general | solution.py:172
  65.1 3.8 %fusion.78 = f32[4,2048]{1,0:T(4,128)S(1)} fusion(s32[1024]{0:T(1024)S(1)} %iota_add_fusion.5, s32[2048]{0:T(1024)S(1)} %get-tuple-element.723, f32[4,2048]{1,0:T(4,128)S(1)} %get-tuple-element.713, f32[4,4096]{1,0:T(4,128)S(1)} %get-tuple-element.722, s32[]{:T(128)S(6)} %select_n.107, pred[]{:T(512)S(6)} %compare.10), kind=kOutput, calls=%fused_computation.30.clone.1 | convolution fusion | flops 102776832 | bytes 94213 | tf_op jit(solution)/shard_map/while/body/eval_jaxpr/dot_general | solution.py:172
  68.9 3.8 %fusion.78 = f32[4,2048]{1,0:T(4,128)S(1)} fusion(s32[1024]{0:T(1024)S(1)} %iota_add_fusion.5, s32[2048]{0:T(1024)S(1)} %get-tuple-element.723, f32[4,2048]{1,0:T(4,128)S(1)} %get-tuple-element.713, f32[4,4096]{1,0:T(4,128)S(1)} %get-tuple-element.722, s32[]{:T(128)S(6)} %select_n.107, pred[]{:T(512)S(6)} %compare.10), kind=kOutput, calls=%fused_computation.30.clone.1 | convolution fusion | flops 102776832 | bytes 94213 | tf_op jit(solution)/shard_map/while/body/eval_jaxpr/dot_general | solution.py:172
  72.7 3.8 %fusion.78 = f32[4,2048]{1,0:T(4,128)S(1)} fusion(s32[1024]{0:T(1024)S(1)} %iota_add_fusion.5, s32[2048]{0:T(1024)S(1)} %get-tuple-element.723, f32[4,2048]{1,0:T(4,128)S(1)} %get-tuple-element.713, f32[4,4096]{1,0:T(4,128)S(1)} %get-tuple-element.722, s32[]{:T(128)S(6)} %select_n.107, pred[]{:T(512)S(6)} %compare.10), kind=kOutput, calls=%fused_computation.30.clone.1 | convolution fusion | flops 102776832 | bytes 94213 | tf_op jit(solution)/shard_map/while/body/eval_jaxpr/dot_general | solution.py:172
  (65 shorter events, 4.1 us)
Async XLA Ops:
  13.6 14.7 %all-to-all-start = ((f32[5,8,512]{2,0,1:T(8,128)}), f32[5,8,512]{2,0,1:T(8,128)S(1)}, u32[]{:S(2)}, u32[]{:S(2)}) async-start(f32[5,8,512]{2,0,1:T(8,128)} %pad_maximum_fusion), calls=%async_computation | async-start | bytes 262144 | tf_op jit(solution)/shard_map/all_to_all | solution.py:122
  36.4 5.5 %copy-start = (f32[4,4,1440]{2,1,0:T(4,128)}, f32[4,4,1440]{2,1,0:T(4,128)S(1)}, u32[]{:S(2)}) copy-start(f32[4,4,1440]{2,1,0:T(4,128)S(1)} %get-tuple-element.510) | copy-start | bytes 276484
  41.8 0.6 copy-start.1
  51.1 10.2 %all-to-all-start.1 = ((f32[4,8,512]{2,0,1:T(4,128)}), f32[4,8,512]{2,0,1:T(4,128)S(1)}, u32[]{:S(2)}, u32[]{:S(2)}) async-start(f32[4,8,512]{2,0,1:T(4,128)} %bitcast.12), calls=%async_computation.1 | async-start | bytes 131072 | tf_op jit(solution)/shard_map/all_to_all | solution.py:163
  76.5 0.6 copy-start.2
